TPU v7x, 512 devices: a whole 4x4x16 slice. The times are simulated.
512 devices in a mesh: pt: 64 (over z_hi, x, y), sub: 8 (over z_lo, core).
Axes of the slice: x: 4, y: 4, z: 16 (z_hi: 4, z_lo: 4; z = z_hi * 4 + z_lo), core: 2. Of those that a mesh axis runs over, the one named last changes fastest.
Arguments:
- kernel_diag: bfloat16 [131072, 256], P(('pt', 'sub')), may hold values from -1 to 4
- pair_quads: bfloat16 [2, 131072, 128], P(None, ('pt', 'sub')), may hold values from -0.21875 to 0.21875
- tile_mask: int32 [2, 1024, 1], P(None, ('pt', 'sub')), may hold values 0 or 1
- right_side: float32 [131072, 64], P(('pt', 'sub')), may hold values from -40 to 40
- basis: float32 [131072, 256], P(('pt', 'sub')), may hold values from -1 to 1
- spectrum: float32 [256], replicated, may hold values from 0.25 to 2
Outputs:
- solution: float32 [131072, 64], P(('pt', 'sub'))
- residual: float32 [131072, 64], P(('pt', 'sub'))
All inputs are finite; a program needn't handle non-finite values. No bound on the sum of `tile_mask` on one device may be relied on, other than what follows from the above.
Results may differ from a plain program's by a relative error of at most 0.006.
Values may be sent and summed in bfloat16 or wider, within the bound.
A program may use at most 64 MiB of HBM per device.

v0:
```python
import jax
import jax.numpy as jnp
from jax import lax
from jax.sharding import PartitionSpec as P

ITERS = 2


LOWER = 0.2
UPPER = 12.0


def partner(shard, axis, stride):
    return lax.ppermute(shard, axis, [(i, i ^ 1 << stride) for i in range(lax.axis_size(axis))])


def cut_along(shard, dim, devices):
    before, after = (shard.shape[:dim], shard.shape[dim + 1 :])
    return jnp.moveaxis(shard.reshape(*before, devices, -1, *after), dim, 0)


def sum_at_owner(shard, axis, dim):
    blocks = cut_along(shard, dim, lax.axis_size(axis))
    arrived = lax.all_to_all(blocks, axis, split_axis=0, concat_axis=0, tiled=True)
    return arrived.astype(jnp.float32).sum(axis=0)


def copy_for_each(shard, axis):
    copies = jnp.broadcast_to(shard, (lax.axis_size(axis), *shard.shape))
    return lax.all_to_all(copies, axis, split_axis=0, concat_axis=0, tiled=True)


def taken_together(shard, axis):
    return copy_for_each(shard, axis).sum(axis=0)


def laid_out(blocks, dim):
    blocks = jnp.moveaxis(blocks, 0, dim)
    shape = blocks.shape
    return blocks.reshape(*shape[:dim], shape[dim] * shape[dim + 1], *shape[dim + 2 :])


def gathered_copies(shard, axis, dim):
    return laid_out(copy_for_each(shard, axis), dim)


def reorder(halves, flag):
    return jnp.where(flag == 1, halves[::-1], halves)


def local_products(quad_pair, partner_vec, pair_role):
    return jnp.einsum(
        "jab,jbc->jac",
        quad_pair,
        reorder(partner_vec, pair_role),
        preferred_element_type=jnp.float32,
    )


def transposed_products(quad_pair, vectors):
    return jnp.einsum(
        "jba,jbc->jac", quad_pair, vectors, preferred_element_type=jnp.float32
    ).astype(jnp.bfloat16)


def on_device(kernel_diag, pair_quads, tile_mask, right_side, basis, spectrum):
    row_count = kernel_diag.shape[0]
    half_rows = row_count // 2
    columns = right_side.shape[1]
    rank_count = basis.shape[1]
    tile_size = row_count // tile_mask.shape[1]
    pt_count = lax.axis_size("pt")
    point_total = row_count * pt_count * lax.axis_size("sub")
    pt_index = lax.axis_index("pt")
    far_bit = pt_count.bit_length() - 2
    near_role = jnp.bitwise_and(pt_index, 1)
    far_role = jnp.bitwise_and(jnp.right_shift(pt_index, far_bit), 1)
    ones = jnp.repeat(
        jnp.repeat(tile_mask.astype(jnp.bfloat16), tile_size, axis=1), tile_size, axis=2
    )
    quad_blocks = (pair_quads * ones).reshape(2, 2, half_rows, half_rows)
    near_quads = quad_blocks[0]
    far_quads = quad_blocks[1]
    near_partner = partner(near_quads, "pt", 0)
    far_partner = partner(far_quads, "pt", far_bit)

    def precondition(residual):
        local_coeffs = lax.dot_general(
            basis,
            residual,
            (((0,), (0,)), ((), ())),
            precision=lax.Precision.HIGHEST,
            preferred_element_type=jnp.float32,
        )
        share = sum_at_owner(local_coeffs.astype(jnp.bfloat16), "sub", 0)
        share = taken_together(share, "pt")
        coeffs = gathered_copies(share, "sub", 0)
        scaled = spectrum[:, None] * coeffs
        return 0.5 * residual + rank_count / point_total * jnp.dot(
            basis, scaled, precision=lax.Precision.HIGHEST
        )

    centre = 0.5 * (UPPER + LOWER)
    radius = 0.5 * (UPPER - LOWER)
    aspect = centre / radius
    ratio_now = 1.0 / aspect
    solution = jnp.zeros_like(right_side)
    residual = right_side
    direction = precondition(residual) / centre
    for sweep in range(ITERS):
        direction_bf = direction.astype(jnp.bfloat16)
        solution = solution + direction
        result = jnp.dot(kernel_diag, direction_bf, preferred_element_type=jnp.float32)
        near_vec = partner(direction_bf, "pt", 0).reshape(2, half_rows, columns)
        far_vec = partner(direction_bf, "pt", far_bit).reshape(2, half_rows, columns)
        near_back = transposed_products(near_partner, near_vec)
        far_back = transposed_products(far_partner, far_vec)
        coupled = local_products(near_quads, near_vec, near_role) + reorder(
            near_back, 1 - near_role
        ).astype(jnp.float32)
        coupled = (
            coupled
            + local_products(far_quads, far_vec, far_role)
            + reorder(far_back, 1 - far_role).astype(jnp.float32)
        )
        residual = residual - (result + coupled.reshape(row_count, columns))
        if sweep + 1 < ITERS:
            precond = precondition(residual)
            ratio_next = 1.0 / (2.0 * aspect - ratio_now)
            direction = ratio_next * ratio_now * direction + 2.0 * ratio_next / radius * precond
            ratio_now = ratio_next
    return (solution, residual)


def solution(mesh):
    placed = (
        P(("pt", "sub"), None),
        P(None, ("pt", "sub"), None),
        P(None, ("pt", "sub"), None),
        P(("pt", "sub"), None),
        P(("pt", "sub"), None),
        P(),
    )
    return jax.shard_map(
        on_device,
        mesh=mesh,
        in_specs=placed,
        out_specs=(P(("pt", "sub"), None), P(("pt", "sub"), None)),
        check_vma=False,
    )
```

profile of v0, /device:TPU:1, one launch (start us, length us, event | category | flops | bytes accessed | tf_op | source)
XLA Modules:
  0.0 187.5 jit_solution(17924692446144452336)
XLA Ops:
  0.6 0.9 copy-done
  1.6 1.1 convolution_convert_fusion.5
  2.7 0.1 copy.38
  2.8 0.1 reshape.60
  2.9 14.2 %all_to_all.30 = bf16[8,2,1024]{2,1,0:T(2,128)(2,1)S(1)} all-to-all(bf16[8,2,1024]{2,1,0:T(2,128)(2,1)S(1)} %reshape.60), channel_id=1, replica_groups=mesh['pt'=64,'sub'=8] {'sub'}, dimensions={0} | all-to-all | bytes 65536 | tf_op jit(solution)/shard_map/all_to_all | solution.py:24
  17.4 1.4 reshape.62
  18.8 16.3 %all-to-all-start.1 = ((f32[64,1,2048]{2,1,0:T(1,128)}), f32[64,1,2048]{2,1,0:T(1,128)S(1)}, u32[]{:S(2)}, u32[]{:S(2)}) async-start(f32[64,1,2048]{2,1,0:T(1,128)} %reshape.62), calls=%async_computation.1 | async-start | bytes 1048576 | tf_op jit(solution)/shard_map/all_to_all | solution.py:30
  35.3 30.1 %all-to-all-done.1 = f32[64,1,2048]{2,1,0:T(1,128)S(1)} async-done(((f32[64,1,2048]{2,1,0:T(1,128)}), f32[64,1,2048]{2,1,0:T(1,128)S(1)}, u32[]{:S(2)}, u32[]{:S(2)}) %all-to-all-start.1) | async-done | bytes 524320 | tf_op jit(solution)/shard_map/all_to_all | solution.py:30
  65.4 0.5 broadcast.23
  65.9 1.9 %reduce = f32[64,2048]{1,0:T(8,128)S(1)} reduce(f32[64,1,2048]{2,1,0:T(1,128)S(1)} %all-to-all-done.1, f32[]{:T(128)} %broadcast.23), dimensions={1}, to_apply=%all_to_all.19.reduce_sub_computation | reduce | bytes 1048580 | tf_op jit(solution)/shard_map/all_to_all | solution.py:30
  67.8 0.4 reshape.63
  68.4 0.8 reshape.64
  69.1 8.3 %all-to-all-start.2 = ((f32[8,1,2048]{2,1,0:T(1,128)}), f32[8,1,2048]{2,1,0:T(1,128)S(1)}, u32[]{:S(2)}, u32[]{:S(2)}) async-start(f32[8,1,2048]{2,1,0:T(1,128)} %reshape.64), calls=%async_computation.2 | async-start | bytes 131072 | tf_op jit(solution)/shard_map/all_to_all | solution.py:30
  77.4 0.1 broadcast_multiply_fusion
  77.6 3.2 %collective-permute-start.3 = (bf16[2,128,128]{2,1,0:T(8,128)(2,1)S(1)}, bf16[2,128,128]{2,1,0:T(8,128)(2,1)S(1)}, u32[]{:S(2)}, u32[]{:S(2)}) collective-permute-start(bf16[2,128,128]{2,1,0:T(8,128)(2,1)S(1)} %bitcast.113), channel_id=1, source_target_pairs={{0,256},{8,264},{16,272},{24,280},{32,288},{40,296},{48,304},{56,3... | collective-permute-start | bytes 196616 | tf_op jit(solution)/shard_map/ppermute | solution.py:14
  80.8 1.7 all-to-all-done.2
  82.5 0.8 reduce.1
  83.4 0.6 copy-done.4
  84.1 0.7 copy-done.1
  84.8 0.4 multiply_convert_fusion
  85.2 9.1 %collective-permute-start.2 = (bf16[256,64]{0,1:T(8,128)(2,1)S(1)}, bf16[256,64]{0,1:T(8,128)(2,1)S(1)}, u32[]{:S(2)}, u32[]{:S(2)}) collective-permute-start(bf16[256,64]{0,1:T(8,128)(2,1)S(1)} %get-tuple-element.6), channel_id=1, source_target_pairs={{0,256},{8,264},{16,272},{24,280},{32,288},{40,296},{48,304},{56,3... | collective-permute-start | bytes 98312 | tf_op jit(solution)/shard_map/ppermute | solution.py:14
  94.3 2.3 %collective-permute-start.1 = (bf16[2,128,128]{2,1,0:T(8,128)(2,1)S(1)}, bf16[2,128,128]{2,1,0:T(8,128)(2,1)S(1)}, u32[]{:S(2)}, u32[]{:S(2)}) collective-permute-start(bf16[2,128,128]{2,1,0:T(8,128)(2,1)S(1)} %bitcast.110), channel_id=1, source_target_pairs={{0,8},{8,0},{16,24},{24,16},{32,40},{40,32},{48,56},{56,48},{64,72... | collective-permute-start | bytes 196616 | tf_op jit(solution)/shard_map/ppermute | solution.py:14
  96.6 3.0 %collective-permute-start = (bf16[256,64]{0,1:T(8,128)(2,1)S(1)}, bf16[256,64]{0,1:T(8,128)(2,1)S(1)}, u32[]{:S(2)}, u32[]{:S(2)}) collective-permute-start(bf16[256,64]{0,1:T(8,128)(2,1)S(1)} %get-tuple-element.6), channel_id=1, source_target_pairs={{0,8},{8,0},{16,24},{24,16},{32,40},{40,32},{48,56},{56,48},{64,72... | collective-permute-start | bytes 98312 | tf_op jit(solution)/shard_map/ppermute | solution.py:14
  99.6 0.1 convolution_convert_fusion.2
  99.8 1.4 collective-permute-done
  101.3 0.1 convolution_convert_fusion.3
  101.5 0.1 convolution_add_fusion.3
  101.6 0.1 fusion.5
  101.8 0.7 copy-done.2
  102.5 0.2 fusion.7
  102.7 0.3 fusion.14
  103.2 11.9 %all_to_all.31 = bf16[8,2,1024]{2,1,0:T(2,128)(2,1)S(1)} all-to-all(bf16[8,2,1024]{2,1,0:T(2,128)(2,1)S(1)} %reshape.66), channel_id=1, replica_groups=mesh['pt'=64,'sub'=8] {'sub'}, dimensions={0} | all-to-all | bytes 65536 | tf_op jit(solution)/shard_map/all_to_all | solution.py:24
  115.3 0.7 reshape.68
  116.0 38.9 %all_to_all.32 = f32[64,1,2048]{2,1,0:T(1,128)S(1)} all-to-all(f32[64,1,2048]{2,1,0:T(1,128)S(1)} %reshape.68), channel_id=1, replica_groups=mesh['pt'=64,'sub'=8] {'pt'}, dimensions={0} | all-to-all | bytes 1048576 | tf_op jit(solution)/shard_map/all_to_all | solution.py:30
  154.9 1.9 %reduce.2 = f32[64,2048]{1,0:T(8,128)S(1)} reduce(f32[64,1,2048]{2,1,0:T(1,128)S(1)} %all_to_all.32, f32[]{:T(128)} %broadcast.23), dimensions={1}, to_apply=%all_to_all.22.reduce_sub_computation | reduce | bytes 1048580 | tf_op jit(solution)/shard_map/all_to_all | solution.py:30
  156.8 0.4 reshape.69
  157.4 0.1 reshape.70
  157.5 13.2 %all_to_all.33 = f32[8,1,2048]{2,1,0:T(1,128)S(1)} all-to-all(f32[8,1,2048]{2,1,0:T(1,128)S(1)} %reshape.70), channel_id=1, replica_groups=mesh['pt'=64,'sub'=8] {'sub'}, dimensions={0} | all-to-all | bytes 131072 | tf_op jit(solution)/shard_map/all_to_all | solution.py:30
  170.6 0.8 reduce.3
  171.6 1.0 fusion.16
  172.7 3.2 %collective-permute-start.5 = (bf16[256,64]{0,1:T(8,128)(2,1)S(1)}, bf16[256,64]{0,1:T(8,128)(2,1)S(1)}, u32[]{:S(2)}, u32[]{:S(2)}) collective-permute-start(bf16[256,64]{0,1:T(8,128)(2,1)S(1)} %get-tuple-element.4), channel_id=1, source_target_pairs={{0,256},{8,264},{16,272},{24,280},{32,288},{40,296},{48,304},{56,3... | collective-permute-start | bytes 98312 | tf_op jit(solution)/shard_map/ppermute | solution.py:14
  175.9 2.2 %collective-permute-start.4 = (bf16[256,64]{0,1:T(8,128)(2,1)S(1)}, bf16[256,64]{0,1:T(8,128)(2,1)S(1)}, u32[]{:S(2)}, u32[]{:S(2)}) collective-permute-start(bf16[256,64]{0,1:T(8,128)(2,1)S(1)} %get-tuple-element.4), channel_id=1, source_target_pairs={{0,8},{8,0},{16,24},{24,16},{32,40},{40,32},{48,56},{56,48},{64,72... | collective-permute-start | bytes 98312 | tf_op jit(solution)/shard_map/ppermute | solution.py:14
  178.1 8.0 %collective-permute-done.5 = bf16[256,64]{0,1:T(8,128)(2,1)S(1)} collective-permute-done((bf16[256,64]{0,1:T(8,128)(2,1)S(1)}, bf16[256,64]{0,1:T(8,128)(2,1)S(1)}, u32[]{:S(2)}, u32[]{:S(2)}) %collective-permute-start.5) | collective-permute-done | bytes 32800 | tf_op jit(solution)/shard_map/ppermute | solution.py:14
  186.0 0.1 convolution_convert_fusion
  186.2 0.1 convolution_convert_fusion.1
  186.4 0.1 convolution_add_fusion.1
  186.5 0.2 fusion.1
  186.7 0.8 fusion.3
  (43 shorter events, 1.6 us)
Async XLA Ops:
  0.6 1.0 copy-start
  18.8 16.3 %copy-start.5 = (s32[2,2,1]{1,2,0:T(1,128)S(1)}, s32[2,2,1]{1,2,0:T(1,128)}, u32[]{:S(2)}) copy-start(s32[2,2,1]{1,2,0:T(1,128)} %param.8) | copy-start | bytes 52
  18.8 46.6 %all-to-all-start.1 = ((f32[64,1,2048]{2,1,0:T(1,128)}), f32[64,1,2048]{2,1,0:T(1,128)S(1)}, u32[]{:S(2)}, u32[]{:S(2)}) async-start(f32[64,1,2048]{2,1,0:T(1,128)} %reshape.62), calls=%async_computation.1 | async-start | bytes 1048576 | tf_op jit(solution)/shard_map/all_to_all | solution.py:30
  68.3 9.1 %copy-start.3 = (bf16[2,256,128]{2,1,0:T(8,128)(2,1)S(1)}, bf16[2,256,128]{2,1,0:T(8,128)(2,1)}, u32[]{:S(2)}) copy-start(bf16[2,256,128]{2,1,0:T(8,128)(2,1)} %param.7) | copy-start | bytes 393220
  69.1 13.4 %all-to-all-start.2 = ((f32[8,1,2048]{2,1,0:T(1,128)}), f32[8,1,2048]{2,1,0:T(1,128)S(1)}, u32[]{:S(2)}, u32[]{:S(2)}) async-start(f32[8,1,2048]{2,1,0:T(1,128)} %reshape.64), calls=%async_computation.2 | async-start | bytes 131072 | tf_op jit(solution)/shard_map/all_to_all | solution.py:30
  77.6 22.1 %collective-permute-start.3 = (bf16[2,128,128]{2,1,0:T(8,128)(2,1)S(1)}, bf16[2,128,128]{2,1,0:T(8,128)(2,1)S(1)}, u32[]{:S(2)}, u32[]{:S(2)}) collective-permute-start(bf16[2,128,128]{2,1,0:T(8,128)(2,1)S(1)} %bitcast.113), channel_id=1, source_target_pairs={{0,256},{8,264},{16,272},{24,280},{32,288},{40,296},{48,304},{56,3... | collective-permute-start | bytes 196616 | tf_op jit(solution)/shard_map/ppermute | solution.py:14
  83.3 0.7 copy-start.4
  84.0 0.8 copy-start.1
  85.2 14.5 %collective-permute-start.2 = (bf16[256,64]{0,1:T(8,128)(2,1)S(1)}, bf16[256,64]{0,1:T(8,128)(2,1)S(1)}, u32[]{:S(2)}, u32[]{:S(2)}) collective-permute-start(bf16[256,64]{0,1:T(8,128)(2,1)S(1)} %get-tuple-element.6), channel_id=1, source_target_pairs={{0,256},{8,264},{16,272},{24,280},{32,288},{40,296},{48,304},{56,3... | collective-permute-start | bytes 98312 | tf_op jit(solution)/shard_map/ppermute | solution.py:14
  94.3 5.5 %collective-permute-start.1 = (bf16[2,128,128]{2,1,0:T(8,128)(2,1)S(1)}, bf16[2,128,128]{2,1,0:T(8,128)(2,1)S(1)}, u32[]{:S(2)}, u32[]{:S(2)}) collective-permute-start(bf16[2,128,128]{2,1,0:T(8,128)(2,1)S(1)} %bitcast.110), channel_id=1, source_target_pairs={{0,8},{8,0},{16,24},{24,16},{32,40},{40,32},{48,56},{56,48},{64,72... | collective-permute-start | bytes 196616 | tf_op jit(solution)/shard_map/ppermute | solution.py:14
  96.6 4.7 %collective-permute-start = (bf16[256,64]{0,1:T(8,128)(2,1)S(1)}, bf16[256,64]{0,1:T(8,128)(2,1)S(1)}, u32[]{:S(2)}, u32[]{:S(2)}) collective-permute-start(bf16[256,64]{0,1:T(8,128)(2,1)S(1)} %get-tuple-element.6), channel_id=1, source_target_pairs={{0,8},{8,0},{16,24},{24,16},{32,40},{40,32},{48,56},{56,48},{64,72... | collective-permute-start | bytes 98312 | tf_op jit(solution)/shard_map/ppermute | solution.py:14
  101.6 0.9 copy-start.2
  172.7 13.4 %collective-permute-start.5 = (bf16[256,64]{0,1:T(8,128)(2,1)S(1)}, bf16[256,64]{0,1:T(8,128)(2,1)S(1)}, u32[]{:S(2)}, u32[]{:S(2)}) collective-permute-start(bf16[256,64]{0,1:T(8,128)(2,1)S(1)} %get-tuple-element.4), channel_id=1, source_target_pairs={{0,256},{8,264},{16,272},{24,280},{32,288},{40,296},{48,304},{56,3... | collective-permute-start | bytes 98312 | tf_op jit(solution)/shard_map/ppermute | solution.py:14
  175.9 10.3 %collective-permute-start.4 = (bf16[256,64]{0,1:T(8,128)(2,1)S(1)}, bf16[256,64]{0,1:T(8,128)(2,1)S(1)}, u32[]{:S(2)}, u32[]{:S(2)}) collective-permute-start(bf16[256,64]{0,1:T(8,128)(2,1)S(1)} %get-tuple-element.4), channel_id=1, source_target_pairs={{0,8},{8,0},{16,24},{24,16},{32,40},{40,32},{48,56},{56,48},{64,72... | collective-permute-start | bytes 98312 | tf_op jit(solution)/shard_map/ppermute | solution.py:14
where the time goes:
time: 189 us; the launch traced here: 188 us
  blocking collectives  78.1 us (41%)
  starting transfers between devices  47.6 us (25%)
  waiting for transfers between devices  41.2 us (22%)
  local copies, waits for them, and re-layouts  8.59 us (5%)
  other arithmetic  6.02 us (3%)
  matrix products  4.87 us (3%)
    all_to_all x2, blocking collectives, copy_for_each(): return lax.all_to_all(copies, axis, split_axis=0, concat_axis=0, tiled=True)  52.1 us
    all_to_all x2, waiting for transfers between devices, copy_for_each(): return lax.all_to_all(copies, axis, split_axis=0, concat_axis=0, tiled=True)  31.8 us
    all_to_all x2, blocking collectives, sum_at_owner(): lax.all_to_all(blocks, axis, split_axis=0, concat_axis=0, tiled=True)  26 us
    all_to_all x2, starting transfers between devices, copy_for_each(): return lax.all_to_all(copies, axis, split_axis=0, concat_axis=0, tiled=True)  24.6 us
    ppermute x6, starting transfers between devices, partner(): lax.ppermute(shard, axis, [(i, i ^ 1 << stride) for i in range(lax.axis_s...  23 us
    ppermute x6, waiting for transfers between devices, partner(): lax.ppermute(shard, axis, [(i, i ^ 1 << stride) for i in range(lax.axis_s...  9.41 us
    unnamed x27, local copies, waits for them, and re-layouts  7.56 us
    all_to_all x4, other arithmetic, copy_for_each(): return lax.all_to_all(copies, axis, split_axis=0, concat_axis=0, tiled=True)  5.36 us
  transfers between devices with their start and end apart: 8, of which 4 were waited for; matrix products, arithmetic and copies ran while one was open for 1% of the time, Pallas kernels for 0%

commit v1 on v0

v1 whole, which is shorter than its diff:
```python
import jax
import jax.numpy as jnp
from jax import lax
from jax.experimental import pallas as pl
from jax.experimental.pallas import tpu as pltpu
from jax.sharding import PartitionSpec as P

ITERS = 2
LOWER = 0.2
UPPER = 12.0
ROWS = 256
HALF = 128
RHS = 64
RANK = 256
N_PT = 64
N_SUB = 8
POINTS = ROWS * N_PT * N_SUB
PLANE = 32
CHIPS = 16
RING = 16
PIECE = (4, 128)
MESH = pl.DeviceIdType.MESH
F32 = jnp.float32
BF16 = jnp.bfloat16


def split(value):
    high = value.astype(BF16)
    return high, (value - high.astype(F32)).astype(BF16)


def dot_nn(left, right):
    return lax.dot_general(left, right, (((1,), (0,)), ((), ())), preferred_element_type=F32)


def dot_nt(left, right):
    return lax.dot_general(left, right, (((1,), (1,)), ((), ())), preferred_element_type=F32)


def send(src, dst, send_sem, recv_sem, device):
    return pltpu.make_async_remote_copy(
        src_ref=src,
        dst_ref=dst,
        send_sem=send_sem,
        recv_sem=recv_sem,
        device_id=device,
        device_id_type=MESH,
    )


def body(
    mask_ref,
    diag_hbm,
    quads_hbm,
    right_hbm,
    basis_hbm,
    spectrum_ref,
    solution_ref,
    residual_ref,
    diag,
    quads,
    right,
    basis,
    basis_hi,
    basis_lo,
    own_quads,
    partner_quads,
    field,
    partner_field,
    coeffs,
    part,
    plane_in,
    plane_sum,
    ring_in,
    ring_sum,
    gathered,
    load_sems,
    quad_send,
    quad_recv,
    field_send,
    field_recv,
    sum_send,
    sum_recv,
):
    pt = lax.axis_index("pt")
    sub = lax.axis_index("sub")
    spot = lax.rem(pt, CHIPS)
    core = lax.rem(sub, 2)
    z_hi = lax.div(pt, CHIPS)
    z_lo = lax.div(sub, 2)
    place = spot * 2 + core
    level = z_hi * 4 + z_lo

    def plane_peer(index):
        return (z_hi * CHIPS + lax.div(index, 2), z_lo * 2 + lax.rem(index, 2))

    def ring_peer(index):
        return (lax.div(index, 4) * CHIPS + spot, lax.rem(index, 4) * 2 + core)

    near_role = lax.rem(pt, 2)
    far_role = lax.div(pt, N_PT // 2)
    partners = (
        (pt + 1 - 2 * near_role, sub),
        (lax.rem(pt + N_PT // 2, N_PT), sub),
    )
    roles = (near_role, far_role)

    loads = [
        pltpu.make_async_copy(src, dst, load_sems.at[i])
        for i, (src, dst) in enumerate(
            ((right_hbm, right), (basis_hbm, basis), (quads_hbm, quads), (diag_hbm, diag))
        )
    ]
    for load in loads:
        load.start()

    barrier = pltpu.get_barrier_semaphore()

    def greet_ring(k, carry):
        pl.semaphore_signal(
            barrier, inc=1, device_id=ring_peer(lax.rem(level + k, RING)), device_id_type=MESH
        )
        return carry

    def greet_plane(k, carry):
        pl.semaphore_signal(
            barrier, inc=1, device_id=plane_peer(lax.rem(place + k, PLANE)), device_id_type=MESH
        )
        return carry

    lax.fori_loop(1, RING, greet_ring, 0)
    lax.fori_loop(1, PLANE, greet_plane, 0)

    def put_part(turn, value):
        coeffs[...] = value
        for i in range(PLANE):
            row, lane = 4 * (i % 16), 128 * (i // 16)
            part[turn, i] = coeffs[row : row + 4, lane : lane + 128]

    def coeff_part(residual):
        high, low = split(residual)
        both = dot_nn(jnp.concatenate([high, low], axis=0), basis_hi[...])
        return both[:RHS] + both[RHS:] + dot_nn(high, basis_lo[...])

    def spread(turn):
        me = part.at[turn]

        def scatter(k, carry):
            peer = lax.rem(place + k, PLANE)
            send(
                me.at[peer],
                plane_in.at[turn, place],
                sum_send.at[turn, 0],
                sum_recv.at[turn, 0],
                plane_peer(peer),
            ).start()
            return carry

        lax.fori_loop(1, PLANE, scatter, 0)
        plane_in[turn, place] = part[turn, place]

    def all_of(ref, count, turn, stage, device):
        span = ref.at[turn, pl.ds(0, count)]
        return send(span, span, sum_send.at[turn, stage], sum_recv.at[turn, stage], device)

    def finish_sum(turn):
        all_of(plane_in, PLANE - 1, turn, 0, partners[0]).wait_recv()
        plane_sum[turn] = jnp.sum(plane_in[turn], axis=0)

        def along(k, carry):
            send(
                plane_sum.at[turn],
                ring_in.at[turn, level],
                sum_send.at[turn, 1],
                sum_recv.at[turn, 1],
                ring_peer(lax.rem(level + k, RING)),
            ).start()
            return carry

        lax.fori_loop(RING // 2, RING, along, 0)
        lax.fori_loop(1, RING // 2, along, 0)
        ring_in[turn, level] = plane_sum[turn]
        all_of(ring_in, RING - 1, turn, 1, partners[0]).wait_recv()
        ring_sum[turn] = jnp.sum(ring_in[turn], axis=0)

        def gather(k, carry):
            send(
                ring_sum.at[turn],
                gathered.at[turn, place],
                sum_send.at[turn, 2],
                sum_recv.at[turn, 2],
                plane_peer(lax.rem(place + k, PLANE)),
            ).start()
            return carry

        lax.fori_loop(1, PLANE, gather, 0)
        gathered[turn, place] = ring_sum[turn]
        all_of(gathered, PLANE - 1, turn, 2, partners[0]).wait_recv()
        for i in range(PLANE):
            row, lane = 4 * (i % 16), 128 * (i // 16)
            coeffs[row : row + 4, lane : lane + 128] = gathered[turn, i]
        return coeffs[...]

    def precondition(residual, summed):
        high, low = split(spectrum_ref[...] * summed)
        both = dot_nt(jnp.concatenate([high, low], axis=0), basis_hi[...])
        term = both[:RHS] + both[RHS:] + dot_nt(high, basis_lo[...])
        return 0.5 * residual + (ROWS / POINTS) * term

    def field_copy(turn, m):
        return send(
            field.at[turn],
            partner_field.at[turn, m],
            field_send.at[turn, m],
            field_recv.at[turn, m],
            partners[m],
        )

    def quad_copy(m):
        return send(
            own_quads.at[m], partner_quads.at[m], quad_send.at[m], quad_recv.at[m], partners[m]
        )

    loads[0].wait()
    residual = right[...].T
    loads[1].wait()
    high, low = split(basis[...])
    basis_hi[...] = high
    basis_lo[...] = low
    put_part(0, coeff_part(residual))
    loads[2].wait()
    for m in range(2):
        for j in range(2):
            keep = mask_ref[m, j, 0].astype(F32)
            rows = quads[m, j * HALF : (j + 1) * HALF, :].astype(F32)
            own_quads[m, j] = (rows * keep).astype(BF16)
    pl.semaphore_wait(barrier, PLANE + RING - 2)

    spread(0)
    for m in range(2):
        quad_copy(m).start()
    loads[3].wait()

    centre = 0.5 * (UPPER + LOWER)
    radius = 0.5 * (UPPER - LOWER)
    aspect = centre / radius
    ratio_now = 1.0 / aspect
    direction = precondition(residual, finish_sum(0)) / centre
    solution = jnp.zeros_like(direction)
    for sweep in range(ITERS):
        direction_bf = direction.astype(BF16)
        field[sweep, 0] = direction_bf[:, :HALF]
        field[sweep, 1] = direction_bf[:, HALF:]
        for m in (1, 0):
            field_copy(sweep, m).start()
        solution = solution + direction
        result = dot_nt(direction_bf, diag[...])
        for m in range(2):
            if sweep == 0:
                quad_copy(m).wait_recv()
            field_copy(sweep, m).wait_recv()
            halves = []
            for j in range(2):
                same = j + roles[m] - 2 * j * roles[m]
                other = 1 - same
                halves.append(
                    dot_nt(partner_field[sweep, m, same], own_quads[m, j])
                    + dot_nn(partner_field[sweep, m, other], partner_quads[m, other])
                )
            result = result + jnp.concatenate(halves, axis=1)
        residual = residual - result
        if sweep + 1 < ITERS:
            put_part(sweep + 1, coeff_part(residual))
            spread(sweep + 1)
            summed = finish_sum(sweep + 1)
            precond = precondition(residual, summed)
            ratio_next = 1.0 / (2.0 * aspect - ratio_now)
            direction = ratio_next * ratio_now * direction + 2.0 * ratio_next / radius * precond
            ratio_now = ratio_next
    solution_ref[...] = solution.T
    residual_ref[...] = residual.T

    for m in range(2):
        quad_copy(m).wait_send()
    for turn in range(ITERS):
        for m in range(2):
            field_copy(turn, m).wait_send()
        all_of(plane_in, PLANE - 1, turn, 0, partners[0]).wait_send()
        all_of(ring_in, RING - 1, turn, 1, partners[0]).wait_send()
        all_of(gathered, PLANE - 1, turn, 2, partners[0]).wait_send()


def on_device(kernel_diag, pair_quads, tile_mask, right_side, basis, spectrum):
    any_spec = pl.BlockSpec(memory_space=pl.ANY)
    vmem_spec = pl.BlockSpec(memory_space=pltpu.VMEM)
    smem_spec = pl.BlockSpec(memory_space=pltpu.SMEM)
    out = jax.ShapeDtypeStruct((ROWS, RHS), F32)
    dma = pltpu.SemaphoreType.DMA
    return pl.pallas_call(
        body,
        name="chebyshev",
        out_shape=(out, out),
        in_specs=[smem_spec, any_spec, any_spec, any_spec, any_spec, vmem_spec],
        out_specs=(vmem_spec, vmem_spec),
        scratch_shapes=[
            pltpu.VMEM((ROWS, ROWS), BF16),
            pltpu.VMEM((2, ROWS, HALF), BF16),
            pltpu.VMEM((ROWS, RHS), F32),
            pltpu.VMEM((ROWS, RANK), F32),
            pltpu.VMEM((ROWS, RANK), BF16),
            pltpu.VMEM((ROWS, RANK), BF16),
            pltpu.VMEM((2, 2, HALF, HALF), BF16),
            pltpu.VMEM((2, 2, HALF, HALF), BF16),
            pltpu.VMEM((ITERS, 2, RHS, HALF), BF16),
            pltpu.VMEM((ITERS, 2, 2, RHS, HALF), BF16),
            pltpu.VMEM((RHS, RANK), F32),
            pltpu.VMEM((ITERS, PLANE, *PIECE), F32),
            pltpu.VMEM((ITERS, PLANE, *PIECE), F32),
            pltpu.VMEM((ITERS, *PIECE), F32),
            pltpu.VMEM((ITERS, RING, *PIECE), F32),
            pltpu.VMEM((ITERS, *PIECE), F32),
            pltpu.VMEM((ITERS, PLANE, *PIECE), F32),
            dma((4,)),
            dma((2,)),
            dma((2,)),
            dma((ITERS, 2)),
            dma((ITERS, 2)),
            dma((ITERS, 3)),
            dma((ITERS, 3)),
        ],
        compiler_params=pltpu.CompilerParams(collective_id=0, has_side_effects=True),
    )(tile_mask, kernel_diag, pair_quads, right_side, basis, spectrum.reshape(1, RANK))


def solution(mesh):
    placed = (
        P(("pt", "sub"), None),
        P(None, ("pt", "sub"), None),
        P(None, ("pt", "sub"), None),
        P(("pt", "sub"), None),
        P(("pt", "sub"), None),
        P(),
    )
    return jax.shard_map(
        on_device,
        mesh=mesh,
        in_specs=placed,
        out_specs=(P(("pt", "sub"), None), P(("pt", "sub"), None)),
        check_vma=False,
    )
```

time: 189 us -> 79.5 us (0.42)
  blocking collectives: 78.1 us -> 0 us
  Pallas kernels: 0 us -> 73.3 us
  starting transfers between devices: 47.6 us -> 0 us
  waiting for transfers between devices: 41.2 us -> 0 us
  other arithmetic: 6.02 us -> 0 us
  matrix products: 4.87 us -> 0 us
  local copies, waits for them, and re-layouts: 8.59 us -> 5.29 us
    all_to_all x4 -> x0, blocking collectives: 78.1 us -> none  [the longest x2 52.1 us: copy_for_each(): return lax.all_to_all(copies, axis, split_axis=0, concat_axis=0, tiled=True)]
    pallas_call x0 -> x1, Pallas kernels: none -> 73.3 us  [on_device(): pl.pallas_call(body, name='chebyshev', out_shape=(out, out), in_specs=[sm...]
    all_to_all x2 -> x0, waiting for transfers between devices: 31.8 us -> none  [copy_for_each(): return lax.all_to_all(copies, axis, split_axis=0, concat_axis=0, tiled=True)]
    all_to_all x2 -> x0, starting transfers between devices: 24.6 us -> none  [copy_for_each(): return lax.all_to_all(copies, axis, split_axis=0, concat_axis=0, tiled=True)]
    ppermute x6 -> x0, starting transfers between devices: 23 us -> none  [partner(): lax.ppermute(shard, axis, [(i, i ^ 1 << stride) for i in range(lax.axis_s...]
    ppermute x6 -> x0, waiting for transfers between devices: 9.41 us -> none  [partner(): lax.ppermute(shard, axis, [(i, i ^ 1 << stride) for i in range(lax.axis_s...]
    all_to_all x4 -> x0, other arithmetic: 5.36 us -> none  [copy_for_each(): return lax.all_to_all(copies, axis, split_axis=0, concat_axis=0, tiled=True)]
    dot_general x14 -> x0, matrix products: 4.87 us -> none  [the longest x2 1.4 us: precondition(): lax.dot_general(basis, residual, (((0,), (0,)), ((), ())), precision=lax....]
  transfers between devices with their start and end apart: 8 -> 0, of which waited for: 4 -> 0; matrix products, arithmetic and copies ran while one was open for 1% -> 0% of each run, Pallas kernels for 0% -> 0%
where the time goes in v1:
time: 79.5 us; the launch traced here: 79.2 us
  Pallas kernels  73.3 us (92%)
  local copies, waits for them, and re-layouts  5.29 us (7%)
    pallas_call x1, Pallas kernels, on_device(): pl.pallas_call(body, name='chebyshev', out_shape=(out, out), in_specs=[sm...  73.3 us
    unnamed x6, local copies, waits for them, and re-layouts  2.93 us
    pallas_call x2, local copies, waits for them, and re-layouts, on_device(): pl.pallas_call(body, name='chebyshev', out_shape=(out, out), in_specs=[sm...  2.36 us

profile of v1, /device:TPU:1, one launch (start us, length us, event | category | flops | bytes accessed | tf_op | source)
XLA Modules:
  0.0 79.2 jit_solution(17270034987873421076)
XLA Ops:
  0.6 0.0 copy-start.1
  0.6 0.7 copy-done.1
  1.3 0.7 copy.8.mask_ref
  2.0 1.6 %copy.9.right_hbm = f32[256,64]{1,0:T(8,128)} copy(f32[256,64]{0,1:T(8,128)} %param.9) | data formatting | bytes 131072 | tf_op args[3]
  3.6 73.3 %chebyshev.1 = (f32[256,64]{1,0:T(8,128)}, f32[256,64]{1,0:T(8,128)}) custom-call(s32[2,2,1]{2,1,0:T(2,128)} %copy.8.mask_ref, bf16[256,256]{1,0:T(8,128)(2,1)} %diag_hbm.1, bf16[2,256,128]{2,1,0:T(8,128)(2,1)} %quads_hbm.1, f32[256,64]{1,0:T(8,128)} %copy.9.right_hbm, f32[256,256]{1,0:T(8,128)} %basis_hbm.1, f32[1,256]{1,0:T(1,128)} %bitcast.1), custom_call_target="tpu_custom_call" | custom-call | tf_op jit(solution)/shard_map/chebyshev/pallas_call | solution.py:299
  76.8 0.0 copy-start
  76.9 1.7 %copy.10 = f32[256,64]{0,1:T(8,128)} copy(f32[256,64]{1,0:T(8,128)} %get-tuple-element.2) | data formatting | bytes 131072 | tf_op jit(solution)/shard_map/chebyshev/pallas_call | solution.py:299
  78.5 0.0 copy-done
  78.5 0.7 copy.11
Async XLA Ops:
  0.6 0.7 copy-start.1
  76.8 1.7 %copy-start = (f32[256,64]{1,0:T(8,128)S(1)}, f32[256,64]{1,0:T(8,128)}, u32[]{:S(2)}) copy-start(f32[256,64]{1,0:T(8,128)} %get-tuple-element.3) | copy-start | bytes 196612

commit v2 on v1

--- a/solution.py
+++ b/solution.py
@@ -222,7 +222,7 @@
         )
 
     loads[0].wait()
-    residual = right[...].T
+    residual = right[...]
     loads[1].wait()
     high, low = split(basis[...])
     basis_hi[...] = high
@@ -231,7 +231,7 @@
     loads[2].wait()
     for m in range(2):
         for j in range(2):
-            keep = mask_ref[m, j, 0].astype(F32)
+            keep = mask_ref[m, 0, j].astype(F32)
             rows = quads[m, j * HALF : (j + 1) * HALF, :].astype(F32)
             own_quads[m, j] = (rows * keep).astype(BF16)
     pl.semaphore_wait(barrier, PLANE + RING - 2)
@@ -277,8 +277,8 @@
             ratio_next = 1.0 / (2.0 * aspect - ratio_now)
             direction = ratio_next * ratio_now * direction + 2.0 * ratio_next / radius * precond
             ratio_now = ratio_next
-    solution_ref[...] = solution.T
-    residual_ref[...] = residual.T
+    solution_ref[...] = solution
+    residual_ref[...] = residual
 
     for m in range(2):
         quad_copy(m).wait_send()
@@ -294,9 +294,9 @@
     any_spec = pl.BlockSpec(memory_space=pl.ANY)
     vmem_spec = pl.BlockSpec(memory_space=pltpu.VMEM)
     smem_spec = pl.BlockSpec(memory_space=pltpu.SMEM)
-    out = jax.ShapeDtypeStruct((ROWS, RHS), F32)
+    out = jax.ShapeDtypeStruct((RHS, ROWS), F32)
     dma = pltpu.SemaphoreType.DMA
-    return pl.pallas_call(
+    solved, left = pl.pallas_call(
         body,
         name="chebyshev",
         out_shape=(out, out),
@@ -305,7 +305,7 @@
         scratch_shapes=[
             pltpu.VMEM((ROWS, ROWS), BF16),
             pltpu.VMEM((2, ROWS, HALF), BF16),
-            pltpu.VMEM((ROWS, RHS), F32),
+            pltpu.VMEM((RHS, ROWS), F32),
             pltpu.VMEM((ROWS, RANK), F32),
             pltpu.VMEM((ROWS, RANK), BF16),
             pltpu.VMEM((ROWS, RANK), BF16),
@@ -329,7 +329,15 @@
             dma((ITERS, 3)),
         ],
         compiler_params=pltpu.CompilerParams(collective_id=0, has_side_effects=True),
-    )(tile_mask, kernel_diag, pair_quads, right_side, basis, spectrum.reshape(1, RANK))
+    )(
+        jnp.swapaxes(tile_mask, 1, 2),
+        kernel_diag,
+        pair_quads,
+        right_side.T,
+        basis,
+        spectrum.reshape(1, RANK),
+    )
+    return solved.T, left.T
 
 
 def solution(mesh):

time: 79.5 us -> 76.1 us (0.957)
  local copies, waits for them, and re-layouts: 5.29 us -> 2.14 us
    pallas_call x2 -> x0, local copies, waits for them, and re-layouts: 2.36 us -> none  [on_device(): pl.pallas_call(body, name='chebyshev', out_shape=(out, out), in_specs=[sm...]
    unnamed x6 -> x4, local copies, waits for them, and re-layouts: 2.93 us -> 2.14 us
where the time goes in v2:
time: 76.1 us; the launch traced here: 75.9 us
  Pallas kernels  73.1 us (96%)
  local copies, waits for them, and re-layouts  2.14 us (3%)
    pallas_call x1, Pallas kernels, on_device(): pl.pallas_call(body, name='chebyshev', out_shape=(out, out), in_specs=[sm...  73.1 us
    unnamed x4, local copies, waits for them, and re-layouts  2.14 us

profile of v2, /device:TPU:1, one launch (start us, length us, event | category | flops | bytes accessed | tf_op | source)
XLA Modules:
  0.0 75.9 jit_solution(825178314069448553)
XLA Ops:
  0.6 73.1 %chebyshev.1 = (f32[64,256]{1,0:T(8,128)}, f32[64,256]{1,0:T(8,128)}) custom-call(s32[2,1,2]{2,1,0:T(1,128)} %bitcast.10, bf16[256,256]{1,0:T(8,128)(2,1)} %diag_hbm.1, bf16[2,256,128]{2,1,0:T(8,128)(2,1)} %quads_hbm.1, f32[64,256]{1,0:T(8,128)} %bitcast.7, f32[256,256]{1,0:T(8,128)} %basis_hbm.1, f32[1,256]{1,0:T(1,128)} %bitcast.11), custom_call_target="tpu_custom_call" | custom-call | tf_op jit(solution)/shard_map/chebyshev/pallas_call | solution.py:299
  73.7 0.0 copy-start
  73.8 1.5 %copy.11 = f32[256,64]{0,1:T(8,128)} copy(f32[256,64]{0,1:T(8,128)} %bitcast.9) | data formatting | bytes 131072
  75.3 0.0 copy-done
  75.3 0.6 copy.12
Async XLA Ops:
  73.7 1.5 %copy-start = (f32[64,256]{1,0:T(8,128)S(1)}, f32[64,256]{1,0:T(8,128)}, u32[]{:S(2)}) copy-start(f32[64,256]{1,0:T(8,128)} %get-tuple-element.5) | copy-start | bytes 196612

commit v3 on v2

--- a/solution.py
+++ b/solution.py
@@ -19,6 +19,7 @@
 CHIPS = 16
 RING = 16
 PIECE = (4, 128)
+CHUNK = 64
 MESH = pl.DeviceIdType.MESH
 F32 = jnp.float32
 BF16 = jnp.bfloat16
@@ -67,6 +68,9 @@
     partner_quads,
     field,
     partner_field,
+    partner_basis,
+    known,
+    partner_known,
     coeffs,
     part,
     plane_in,
@@ -79,6 +83,10 @@
     quad_recv,
     field_send,
     field_recv,
+    basis_send,
+    basis_recv,
+    known_send,
+    known_recv,
     sum_send,
     sum_recv,
 ):
@@ -201,18 +209,19 @@
             coeffs[row : row + 4, lane : lane + 128] = gathered[turn, i]
         return coeffs[...]
 
-    def precondition(residual, summed):
-        high, low = split(spectrum_ref[...] * summed)
-        both = dot_nt(jnp.concatenate([high, low], axis=0), basis_hi[...])
-        term = both[:RHS] + both[RHS:] + dot_nt(high, basis_lo[...])
-        return 0.5 * residual + (ROWS / POINTS) * term
-
-    def field_copy(turn, m):
+    def scaled(summed):
+        return split(ROWS / POINTS * spectrum_ref[...] * summed)
+
+    def low_rank(pair, basis_rows):
+        both = dot_nt(jnp.concatenate(pair, axis=0), basis_rows)
+        return both[:RHS] + both[RHS:]
+
+    def field_copy(m):
         return send(
-            field.at[turn],
-            partner_field.at[turn, m],
-            field_send.at[turn, m],
-            field_recv.at[turn, m],
+            field,
+            partner_field.at[m],
+            field_send.at[m],
+            field_recv.at[m],
             partners[m],
         )
 
@@ -220,6 +229,34 @@
         return send(
             own_quads.at[m], partner_quads.at[m], quad_send.at[m], quad_recv.at[m], partners[m]
         )
+
+    def basis_copy(m, chunk):
+        rows = pl.ds(chunk * CHUNK, CHUNK)
+        return send(
+            basis_hi.at[rows],
+            partner_basis.at[m, rows],
+            basis_send.at[m, chunk],
+            basis_recv.at[m, chunk],
+            partners[m],
+        )
+
+    def known_copy(m):
+        return send(known, partner_known.at[m], known_send.at[m], known_recv.at[m], partners[m])
+
+    def put_halves(ref, value):
+        ref[0] = value[:, :HALF]
+        ref[1] = value[:, HALF:]
+
+    def coupled(m):
+        halves = []
+        for j in range(2):
+            same = j + roles[m] - 2 * j * roles[m]
+            other = 1 - same
+            halves.append(
+                dot_nt(partner_field[m, same], own_quads[m, j])
+                + dot_nn(partner_field[m, other], partner_quads[m, other])
+            )
+        return jnp.concatenate(halves, axis=1)
 
     loads[0].wait()
     residual = right[...]
@@ -245,46 +282,53 @@
     radius = 0.5 * (UPPER - LOWER)
     aspect = centre / radius
     ratio_now = 1.0 / aspect
-    direction = precondition(residual, finish_sum(0)) / centre
-    solution = jnp.zeros_like(direction)
-    for sweep in range(ITERS):
-        direction_bf = direction.astype(BF16)
-        field[sweep, 0] = direction_bf[:, :HALF]
-        field[sweep, 1] = direction_bf[:, HALF:]
+    ratio_next = 1.0 / (2.0 * aspect - ratio_now)
+    gain = 2.0 * ratio_next / radius
+    pair = scaled(finish_sum(0))
+    term = low_rank(pair, basis_hi[...]) + dot_nt(pair[0], basis_lo[...])
+    solution = (0.5 * residual + term) / centre
+
+    direction_bf = solution.astype(BF16)
+    put_halves(field, direction_bf)
+    for m in (1, 0):
+        field_copy(m).start()
+    for chunk in range(ROWS // CHUNK):
         for m in (1, 0):
-            field_copy(sweep, m).start()
-        solution = solution + direction
-        result = dot_nt(direction_bf, diag[...])
-        for m in range(2):
-            if sweep == 0:
-                quad_copy(m).wait_recv()
-            field_copy(sweep, m).wait_recv()
-            halves = []
-            for j in range(2):
-                same = j + roles[m] - 2 * j * roles[m]
-                other = 1 - same
-                halves.append(
-                    dot_nt(partner_field[sweep, m, same], own_quads[m, j])
-                    + dot_nn(partner_field[sweep, m, other], partner_quads[m, other])
-                )
-            result = result + jnp.concatenate(halves, axis=1)
-        residual = residual - result
-        if sweep + 1 < ITERS:
-            put_part(sweep + 1, coeff_part(residual))
-            spread(sweep + 1)
-            summed = finish_sum(sweep + 1)
-            precond = precondition(residual, summed)
-            ratio_next = 1.0 / (2.0 * aspect - ratio_now)
-            direction = ratio_next * ratio_now * direction + 2.0 * ratio_next / radius * precond
-            ratio_now = ratio_next
-    solution_ref[...] = solution
+            basis_copy(m, chunk).start()
+    residual = residual - dot_nt(direction_bf, diag[...])
+    for m in range(2):
+        quad_copy(m).wait_recv()
+        field_copy(m).wait_recv()
+        residual = residual - coupled(m)
+
+    put_part(1, coeff_part(residual))
+    spread(1)
+    direction = ratio_next * ratio_now * solution + 0.5 * gain * residual
+    known[...] = direction.astype(BF16)
+    for m in (1, 0):
+        known_copy(m).start()
+    for m in range(2):
+        field_copy(m).wait_send()
+    pair = scaled(finish_sum(1))
+    term = low_rank(pair, basis_hi[...]) + dot_nt(pair[0], basis_lo[...])
+    direction = direction + gain * term
+    solution_ref[...] = solution + direction
+    residual = residual - dot_nt(direction.astype(BF16), diag[...])
+    for m in range(2):
+        for chunk in range(ROWS // CHUNK):
+            basis_copy(m, chunk).wait_recv()
+        known_copy(m).wait_recv()
+        theirs = partner_known[m].astype(F32) + gain * low_rank(pair, partner_basis[m])
+        put_halves(partner_field.at[m], theirs.astype(BF16))
+        residual = residual - coupled(m)
     residual_ref[...] = residual
 
     for m in range(2):
         quad_copy(m).wait_send()
+        known_copy(m).wait_send()
+        for chunk in range(ROWS // CHUNK):
+            basis_copy(m, chunk).wait_send()
     for turn in range(ITERS):
-        for m in range(2):
-            field_copy(turn, m).wait_send()
         all_of(plane_in, PLANE - 1, turn, 0, partners[0]).wait_send()
         all_of(ring_in, RING - 1, turn, 1, partners[0]).wait_send()
         all_of(gathered, PLANE - 1, turn, 2, partners[0]).wait_send()
@@ -311,8 +355,11 @@
             pltpu.VMEM((ROWS, RANK), BF16),
             pltpu.VMEM((2, 2, HALF, HALF), BF16),
             pltpu.VMEM((2, 2, HALF, HALF), BF16),
-            pltpu.VMEM((ITERS, 2, RHS, HALF), BF16),
-            pltpu.VMEM((ITERS, 2, 2, RHS, HALF), BF16),
+            pltpu.VMEM((2, RHS, HALF), BF16),
+            pltpu.VMEM((2, 2, RHS, HALF), BF16),
+            pltpu.VMEM((2, ROWS, RANK), BF16),
+            pltpu.VMEM((RHS, ROWS), BF16),
+            pltpu.VMEM((2, RHS, ROWS), BF16),
             pltpu.VMEM((RHS, RANK), F32),
             pltpu.VMEM((ITERS, PLANE, *PIECE), F32),
             pltpu.VMEM((ITERS, PLANE, *PIECE), F32),
@@ -323,8 +370,12 @@
             dma((4,)),
             dma((2,)),
             dma((2,)),
-            dma((ITERS, 2)),
-            dma((ITERS, 2)),
+            dma((2,)),
+            dma((2,)),
+            dma((2, ROWS // CHUNK)),
+            dma((2, ROWS // CHUNK)),
+            dma((2,)),
+            dma((2,)),
             dma((ITERS, 3)),
             dma((ITERS, 3)),
         ],

time: 76.1 us -> 75.6 us (level)
  no operation moved by 1% of the time
where the time goes in v3:
time: 75.6 us; the launch traced here: 75.4 us
  Pallas kernels  72.6 us (96%)
  local copies, waits for them, and re-layouts  2.14 us (3%)
    pallas_call x1, Pallas kernels, on_device(): pl.pallas_call(body, name='chebyshev', out_shape=(out, out), in_specs=[sm...  72.6 us
    unnamed x4, local copies, waits for them, and re-layouts  2.14 us

profile of v3, /device:TPU:1, one launch (start us, length us, event | category | flops | bytes accessed | tf_op | source)
XLA Modules:
  0.0 75.4 jit_solution(13510441275643530856)
XLA Ops:
  0.6 72.6 %chebyshev.1 = (f32[64,256]{1,0:T(8,128)}, f32[64,256]{1,0:T(8,128)}) custom-call(s32[2,1,2]{2,1,0:T(1,128)} %bitcast.10, bf16[256,256]{1,0:T(8,128)(2,1)} %diag_hbm.1, bf16[2,256,128]{2,1,0:T(8,128)(2,1)} %quads_hbm.1, f32[64,256]{1,0:T(8,128)} %bitcast.7, f32[256,256]{1,0:T(8,128)} %basis_hbm.1, f32[1,256]{1,0:T(1,128)} %bitcast.11), custom_call_target="tpu_custom_call" | custom-call | tf_op jit(solution)/shard_map/chebyshev/pallas_call | solution.py:343
  73.2 0.0 copy-start
  73.2 1.5 %copy.11 = f32[256,64]{0,1:T(8,128)} copy(f32[256,64]{0,1:T(8,128)} %bitcast.9) | data formatting | bytes 131072
  74.7 0.0 copy-done
  74.7 0.6 copy.12
Async XLA Ops:
  73.2 1.5 %copy-start = (f32[64,256]{1,0:T(8,128)S(1)}, f32[64,256]{1,0:T(8,128)}, u32[]{:S(2)}) copy-start(f32[64,256]{1,0:T(8,128)} %get-tuple-element.5) | copy-start | bytes 196612

commit v4 on v3

--- a/solution.py
+++ b/solution.py
@@ -19,10 +19,15 @@
 CHIPS = 16
 RING = 16
 PIECE = (4, 128)
-CHUNK = 64
+FAR_FIRST = 12
 MESH = pl.DeviceIdType.MESH
 F32 = jnp.float32
 BF16 = jnp.bfloat16
+PLANE_TYPE = BF16
+RING_TYPE = BF16
+GATHER_TYPE = F32
+CHUNK = 32
+BASIS_AT = (4, 4)
 
 
 def split(value):
@@ -143,7 +148,7 @@
         coeffs[...] = value
         for i in range(PLANE):
             row, lane = 4 * (i % 16), 128 * (i // 16)
-            part[turn, i] = coeffs[row : row + 4, lane : lane + 128]
+            part[turn, i] = coeffs[row : row + 4, lane : lane + 128].astype(PLANE_TYPE)
 
     def coeff_part(residual):
         high, low = split(residual)
@@ -164,16 +169,17 @@
             ).start()
             return carry
 
-        lax.fori_loop(1, PLANE, scatter, 0)
+        lax.fori_loop(FAR_FIRST, PLANE, scatter, 0)
+        lax.fori_loop(1, FAR_FIRST, scatter, 0)
         plane_in[turn, place] = part[turn, place]
 
     def all_of(ref, count, turn, stage, device):
         span = ref.at[turn, pl.ds(0, count)]
         return send(span, span, sum_send.at[turn, stage], sum_recv.at[turn, stage], device)
 
-    def finish_sum(turn):
+    def finish_sum(turn, meanwhile=None):
         all_of(plane_in, PLANE - 1, turn, 0, partners[0]).wait_recv()
-        plane_sum[turn] = jnp.sum(plane_in[turn], axis=0)
+        plane_sum[turn] = jnp.sum(plane_in[turn].astype(F32), axis=0).astype(RING_TYPE)
 
         def along(k, carry):
             send(
@@ -189,7 +195,7 @@
         lax.fori_loop(1, RING // 2, along, 0)
         ring_in[turn, level] = plane_sum[turn]
         all_of(ring_in, RING - 1, turn, 1, partners[0]).wait_recv()
-        ring_sum[turn] = jnp.sum(ring_in[turn], axis=0)
+        ring_sum[turn] = jnp.sum(ring_in[turn].astype(F32), axis=0).astype(GATHER_TYPE)
 
         def gather(k, carry):
             send(
@@ -201,12 +207,15 @@
             ).start()
             return carry
 
-        lax.fori_loop(1, PLANE, gather, 0)
+        lax.fori_loop(FAR_FIRST, PLANE, gather, 0)
+        lax.fori_loop(1, FAR_FIRST, gather, 0)
         gathered[turn, place] = ring_sum[turn]
+        if meanwhile is not None:
+            meanwhile()
         all_of(gathered, PLANE - 1, turn, 2, partners[0]).wait_recv()
         for i in range(PLANE):
             row, lane = 4 * (i % 16), 128 * (i // 16)
-            coeffs[row : row + 4, lane : lane + 128] = gathered[turn, i]
+            coeffs[row : row + 4, lane : lane + 128] = gathered[turn, i].astype(F32)
         return coeffs[...]
 
     def scaled(summed):
@@ -239,6 +248,12 @@
             basis_recv.at[m, chunk],
             partners[m],
         )
+
+    def send_basis(point):
+        first = sum(BASIS_AT[:point])
+        for chunk in range(first, first + BASIS_AT[point]):
+            for m in (1, 0):
+                basis_copy(m, chunk).start()
 
     def known_copy(m):
         return send(known, partner_known.at[m], known_send.at[m], known_recv.at[m], partners[m])
@@ -274,7 +289,7 @@
     pl.semaphore_wait(barrier, PLANE + RING - 2)
 
     spread(0)
-    for m in range(2):
+    for m in (1, 0):
         quad_copy(m).start()
     loads[3].wait()
 
@@ -284,7 +299,7 @@
     ratio_now = 1.0 / aspect
     ratio_next = 1.0 / (2.0 * aspect - ratio_now)
     gain = 2.0 * ratio_next / radius
-    pair = scaled(finish_sum(0))
+    pair = scaled(finish_sum(0, lambda: send_basis(0)))
     term = low_rank(pair, basis_hi[...]) + dot_nt(pair[0], basis_lo[...])
     solution = (0.5 * residual + term) / centre
 
@@ -292,15 +307,13 @@
     put_halves(field, direction_bf)
     for m in (1, 0):
         field_copy(m).start()
-    for chunk in range(ROWS // CHUNK):
-        for m in (1, 0):
-            basis_copy(m, chunk).start()
     residual = residual - dot_nt(direction_bf, diag[...])
     for m in range(2):
         quad_copy(m).wait_recv()
         field_copy(m).wait_recv()
         residual = residual - coupled(m)
 
+    send_basis(1)
     put_part(1, coeff_part(residual))
     spread(1)
     direction = ratio_next * ratio_now * solution + 0.5 * gain * residual
@@ -361,12 +374,12 @@
             pltpu.VMEM((RHS, ROWS), BF16),
             pltpu.VMEM((2, RHS, ROWS), BF16),
             pltpu.VMEM((RHS, RANK), F32),
-            pltpu.VMEM((ITERS, PLANE, *PIECE), F32),
-            pltpu.VMEM((ITERS, PLANE, *PIECE), F32),
-            pltpu.VMEM((ITERS, *PIECE), F32),
-            pltpu.VMEM((ITERS, RING, *PIECE), F32),
-            pltpu.VMEM((ITERS, *PIECE), F32),
-            pltpu.VMEM((ITERS, PLANE, *PIECE), F32),
+            pltpu.VMEM((ITERS, PLANE, *PIECE), PLANE_TYPE),
+            pltpu.VMEM((ITERS, PLANE, *PIECE), PLANE_TYPE),
+            pltpu.VMEM((ITERS, *PIECE), RING_TYPE),
+            pltpu.VMEM((ITERS, RING, *PIECE), RING_TYPE),
+            pltpu.VMEM((ITERS, *PIECE), GATHER_TYPE),
+            pltpu.VMEM((ITERS, PLANE, *PIECE), GATHER_TYPE),
             dma((4,)),
             dma((2,)),
             dma((2,)),

time: 75.6 us -> 68 us (0.90)
  Pallas kernels: 72.6 us -> 65 us
    pallas_call x1, Pallas kernels: 72.6 us -> 65 us  [on_device(): pl.pallas_call(body, name='chebyshev', out_shape=(out, out), in_specs=[sm...]
where the time goes in v4:
time: 68 us; the launch traced here: 67.8 us
  Pallas kernels  65 us (96%)
  local copies, waits for them, and re-layouts  2.14 us (3%)
    pallas_call x1, Pallas kernels, on_device(): pl.pallas_call(body, name='chebyshev', out_shape=(out, out), in_specs=[sm...  65 us
    unnamed x4, local copies, waits for them, and re-layouts  2.14 us

profile of v4, /device:TPU:1, one launch (start us, length us, event | category | flops | bytes accessed | tf_op | source)
XLA Modules:
  0.0 67.8 jit_solution(7187070836146513821)
XLA Ops:
  0.6 65.0 %chebyshev.1 = (f32[64,256]{1,0:T(8,128)}, f32[64,256]{1,0:T(8,128)}) custom-call(s32[2,1,2]{2,1,0:T(1,128)} %bitcast.10, bf16[256,256]{1,0:T(8,128)(2,1)} %diag_hbm.1, bf16[2,256,128]{2,1,0:T(8,128)(2,1)} %quads_hbm.1, f32[64,256]{1,0:T(8,128)} %bitcast.7, f32[256,256]{1,0:T(8,128)} %basis_hbm.1, f32[1,256]{1,0:T(1,128)} %bitcast.11), custom_call_target="tpu_custom_call" | custom-call | tf_op jit(solution)/shard_map/chebyshev/pallas_call | solution.py:356
  65.6 0.0 copy-start
  65.7 1.5 %copy.11 = f32[256,64]{0,1:T(8,128)} copy(f32[256,64]{0,1:T(8,128)} %bitcast.9) | data formatting | bytes 131072
  67.2 0.0 copy-done
  67.2 0.6 copy.12
Async XLA Ops:
  65.6 1.5 %copy-start = (f32[64,256]{1,0:T(8,128)S(1)}, f32[64,256]{1,0:T(8,128)}, u32[]{:S(2)}) copy-start(f32[64,256]{1,0:T(8,128)} %get-tuple-element.5) | copy-start | bytes 196612

commit v5 on v4

--- a/solution.py
+++ b/solution.py
@@ -351,7 +351,7 @@
     any_spec = pl.BlockSpec(memory_space=pl.ANY)
     vmem_spec = pl.BlockSpec(memory_space=pltpu.VMEM)
     smem_spec = pl.BlockSpec(memory_space=pltpu.SMEM)
-    out = jax.ShapeDtypeStruct((RHS, ROWS), F32)
+    out = pltpu.VMEM((RHS, ROWS), F32)
     dma = pltpu.SemaphoreType.DMA
     solved, left = pl.pallas_call(
         body,

time: 68 us -> 66.4 us (0.976)
  local copies, waits for them, and re-layouts: 2.14 us -> 1.26 us
    unnamed x4 -> x2, local copies, waits for them, and re-layouts: 2.14 us -> 1.26 us
where the time goes in v5:
time: 66.4 us; the launch traced here: 66.3 us
  Pallas kernels  64.4 us (97%)
  local copies, waits for them, and re-layouts  1.26 us (2%)
    pallas_call x1, Pallas kernels, on_device(): pl.pallas_call(body, name='chebyshev', out_shape=(out, out), in_specs=[sm...  64.4 us

profile of v5, /device:TPU:1, one launch (start us, length us, event | category | flops | bytes accessed | tf_op | source)
XLA Modules:
  0.0 66.3 jit_solution(13158363952019722747)
XLA Ops:
  0.6 64.4 %chebyshev.1 = (f32[64,256]{1,0:T(8,128)S(1)}, f32[64,256]{1,0:T(8,128)S(1)}) custom-call(s32[2,1,2]{2,1,0:T(1,128)} %bitcast.10, bf16[256,256]{1,0:T(8,128)(2,1)} %diag_hbm.1, bf16[2,256,128]{2,1,0:T(8,128)(2,1)} %quads_hbm.1, f32[64,256]{1,0:T(8,128)} %bitcast.9, f32[256,256]{1,0:T(8,128)} %basis_hbm.1, f32[1,256]{1,0:T(1,128)} %bitcast.11), custom_call_target="tpu_custom_call" | custom-call | tf_op jit(solution)/shard_map/chebyshev/pallas_call | solution.py:356
  65.0 0.6 copy.11
  65.6 0.6 copy.12

commit v6 on v5

--- a/solution.py
+++ b/solution.py
@@ -27,6 +27,7 @@
 RING_TYPE = BF16
 GATHER_TYPE = F32
 CHUNK = 32
+GROUP = 5
 BASIS_AT = (4, 4)
 
 
@@ -41,6 +42,19 @@
 
 def dot_nt(left, right):
     return lax.dot_general(left, right, (((1,), (1,)), ((), ())), preferred_element_type=F32)
+
+
+def each(first, last, action):
+    whole = (last - first) // GROUP
+
+    def group(i, carry):
+        for j in range(GROUP):
+            action(first + i * GROUP + j)
+        return carry
+
+    lax.fori_loop(0, whole, group, 0)
+    for k in range(first + whole * GROUP, last):
+        action(k)
 
 
 def send(src, dst, send_sem, recv_sem, device):
@@ -129,20 +143,18 @@
 
     barrier = pltpu.get_barrier_semaphore()
 
-    def greet_ring(k, carry):
+    def greet_ring(k):
         pl.semaphore_signal(
             barrier, inc=1, device_id=ring_peer(lax.rem(level + k, RING)), device_id_type=MESH
         )
-        return carry
-
-    def greet_plane(k, carry):
+
+    def greet_plane(k):
         pl.semaphore_signal(
             barrier, inc=1, device_id=plane_peer(lax.rem(place + k, PLANE)), device_id_type=MESH
         )
-        return carry
-
-    lax.fori_loop(1, RING, greet_ring, 0)
-    lax.fori_loop(1, PLANE, greet_plane, 0)
+
+    each(1, RING, greet_ring)
+    each(1, PLANE, greet_plane)
 
     def put_part(turn, value):
         coeffs[...] = value
@@ -158,7 +170,7 @@
     def spread(turn):
         me = part.at[turn]
 
-        def scatter(k, carry):
+        def scatter(k):
             peer = lax.rem(place + k, PLANE)
             send(
                 me.at[peer],
@@ -167,21 +179,20 @@
                 sum_recv.at[turn, 0],
                 plane_peer(peer),
             ).start()
-            return carry
-
-        lax.fori_loop(FAR_FIRST, PLANE, scatter, 0)
-        lax.fori_loop(1, FAR_FIRST, scatter, 0)
+
+        each(FAR_FIRST, PLANE, scatter)
+        each(1, FAR_FIRST, scatter)
         plane_in[turn, place] = part[turn, place]
 
     def all_of(ref, count, turn, stage, device):
         span = ref.at[turn, pl.ds(0, count)]
         return send(span, span, sum_send.at[turn, stage], sum_recv.at[turn, stage], device)
 
-    def finish_sum(turn, meanwhile=None):
+    def finish_sum(turn, beside_ring, beside_gather):
         all_of(plane_in, PLANE - 1, turn, 0, partners[0]).wait_recv()
         plane_sum[turn] = jnp.sum(plane_in[turn].astype(F32), axis=0).astype(RING_TYPE)
 
-        def along(k, carry):
+        def along(k):
             send(
                 plane_sum.at[turn],
                 ring_in.at[turn, level],
@@ -189,15 +200,15 @@
                 sum_recv.at[turn, 1],
                 ring_peer(lax.rem(level + k, RING)),
             ).start()
-            return carry
-
-        lax.fori_loop(RING // 2, RING, along, 0)
-        lax.fori_loop(1, RING // 2, along, 0)
+
+        each(RING // 2, RING, along)
+        each(1, RING // 2, along)
+        beside_ring()
         ring_in[turn, level] = plane_sum[turn]
         all_of(ring_in, RING - 1, turn, 1, partners[0]).wait_recv()
         ring_sum[turn] = jnp.sum(ring_in[turn].astype(F32), axis=0).astype(GATHER_TYPE)
 
-        def gather(k, carry):
+        def gather(k):
             send(
                 ring_sum.at[turn],
                 gathered.at[turn, place],
@@ -205,13 +216,11 @@
                 sum_recv.at[turn, 2],
                 plane_peer(lax.rem(place + k, PLANE)),
             ).start()
-            return carry
-
-        lax.fori_loop(FAR_FIRST, PLANE, gather, 0)
-        lax.fori_loop(1, FAR_FIRST, gather, 0)
+
+        each(FAR_FIRST, PLANE, gather)
+        each(1, FAR_FIRST, gather)
         gathered[turn, place] = ring_sum[turn]
-        if meanwhile is not None:
-            meanwhile()
+        beside_gather()
         all_of(gathered, PLANE - 1, turn, 2, partners[0]).wait_recv()
         for i in range(PLANE):
             row, lane = 4 * (i % 16), 128 * (i // 16)
@@ -249,11 +258,15 @@
             partners[m],
         )
 
-    def send_basis(point):
+    def far_basis(point):
         first = sum(BASIS_AT[:point])
         for chunk in range(first, first + BASIS_AT[point]):
-            for m in (1, 0):
-                basis_copy(m, chunk).start()
+            basis_copy(1, chunk).start()
+
+    def near_later():
+        known_copy(0).start()
+        for chunk in range(ROWS // CHUNK):
+            basis_copy(0, chunk).start()
 
     def known_copy(m):
         return send(known, partner_known.at[m], known_send.at[m], known_recv.at[m], partners[m])
@@ -289,8 +302,7 @@
     pl.semaphore_wait(barrier, PLANE + RING - 2)
 
     spread(0)
-    for m in (1, 0):
-        quad_copy(m).start()
+    quad_copy(1).start()
     loads[3].wait()
 
     centre = 0.5 * (UPPER + LOWER)
@@ -299,7 +311,7 @@
     ratio_now = 1.0 / aspect
     ratio_next = 1.0 / (2.0 * aspect - ratio_now)
     gain = 2.0 * ratio_next / radius
-    pair = scaled(finish_sum(0, lambda: send_basis(0)))
+    pair = scaled(finish_sum(0, quad_copy(0).start, lambda: far_basis(0)))
     term = low_rank(pair, basis_hi[...]) + dot_nt(pair[0], basis_lo[...])
     solution = (0.5 * residual + term) / centre
 
@@ -313,16 +325,15 @@
         field_copy(m).wait_recv()
         residual = residual - coupled(m)
 
-    send_basis(1)
+    far_basis(1)
     put_part(1, coeff_part(residual))
     spread(1)
     direction = ratio_next * ratio_now * solution + 0.5 * gain * residual
     known[...] = direction.astype(BF16)
-    for m in (1, 0):
-        known_copy(m).start()
+    known_copy(1).start()
     for m in range(2):
         field_copy(m).wait_send()
-    pair = scaled(finish_sum(1))
+    pair = scaled(finish_sum(1, near_later, lambda: None))
     term = low_rank(pair, basis_hi[...]) + dot_nt(pair[0], basis_lo[...])
     direction = direction + gain * term
     solution_ref[...] = solution + direction

time: 66.4 us -> 66.3 us (level)
  no operation moved by 1% of the time
where the time goes in v6:
time: 66.3 us; the launch traced here: 66.1 us
  Pallas kernels  64.2 us (97%)
  local copies, waits for them, and re-layouts  1.26 us (2%)
    pallas_call x1, Pallas kernels, on_device(): pl.pallas_call(body, name='chebyshev', out_shape=(out, out), in_specs=[sm...  64.2 us

profile of v6, /device:TPU:1, one launch (start us, length us, event | category | flops | bytes accessed | tf_op | source)
XLA Modules:
  0.0 66.1 jit_solution(12691594007371076257)
XLA Ops:
  0.6 64.2 %chebyshev.1 = (f32[64,256]{1,0:T(8,128)S(1)}, f32[64,256]{1,0:T(8,128)S(1)}) custom-call(s32[2,1,2]{2,1,0:T(1,128)} %bitcast.10, bf16[256,256]{1,0:T(8,128)(2,1)} %diag_hbm.1, bf16[2,256,128]{2,1,0:T(8,128)(2,1)} %quads_hbm.1, f32[64,256]{1,0:T(8,128)} %bitcast.9, f32[256,256]{1,0:T(8,128)} %basis_hbm.1, f32[1,256]{1,0:T(1,128)} %bitcast.11), custom_call_target="tpu_custom_call" | custom-call | tf_op jit(solution)/shard_map/chebyshev/pallas_call | solution.py:367
  64.9 0.6 copy.11
  65.5 0.6 copy.12

commit v7 on v6

--- a/solution.py
+++ b/solution.py
@@ -28,7 +28,7 @@
 GATHER_TYPE = F32
 CHUNK = 32
 GROUP = 5
-BASIS_AT = (4, 4)
+BASIS_AT = (4, 1, 3)
 
 
 def split(value):
@@ -319,13 +319,14 @@
     put_halves(field, direction_bf)
     for m in (1, 0):
         field_copy(m).start()
+    far_basis(1)
     residual = residual - dot_nt(direction_bf, diag[...])
     for m in range(2):
         quad_copy(m).wait_recv()
         field_copy(m).wait_recv()
         residual = residual - coupled(m)
 
-    far_basis(1)
+    far_basis(2)
     put_part(1, coeff_part(residual))
     spread(1)
     direction = ratio_next * ratio_now * solution + 0.5 * gain * residual

time: 66.3 us -> 66 us (level)
  no operation moved by 1% of the time
where the time goes in v7:
time: 66 us; the launch traced here: 65.8 us
  Pallas kernels  63.9 us (97%)
  local copies, waits for them, and re-layouts  1.26 us (2%)
    pallas_call x1, Pallas kernels, on_device(): pl.pallas_call(body, name='chebyshev', out_shape=(out, out), in_specs=[sm...  63.9 us

profile of v7, /device:TPU:1, one launch (start us, length us, event | category | flops | bytes accessed | tf_op | source)
XLA Modules:
  0.0 65.8 jit_solution(233791470068928854)
XLA Ops:
  0.6 63.9 %chebyshev.1 = (f32[64,256]{1,0:T(8,128)S(1)}, f32[64,256]{1,0:T(8,128)S(1)}) custom-call(s32[2,1,2]{2,1,0:T(1,128)} %bitcast.10, bf16[256,256]{1,0:T(8,128)(2,1)} %diag_hbm.1, bf16[2,256,128]{2,1,0:T(8,128)(2,1)} %quads_hbm.1, f32[64,256]{1,0:T(8,128)} %bitcast.9, f32[256,256]{1,0:T(8,128)} %basis_hbm.1, f32[1,256]{1,0:T(1,128)} %bitcast.11), custom_call_target="tpu_custom_call" | custom-call | tf_op jit(solution)/shard_map/chebyshev/pallas_call | solution.py:368
  64.5 0.6 copy.11
  65.2 0.6 copy.12

commit v8 on v7

--- a/solution.py
+++ b/solution.py
@@ -69,14 +69,16 @@
 
 
 def body(
-    mask_ref,
+    mask_hbm,
     diag_hbm,
     quads_hbm,
     right_hbm,
     basis_hbm,
-    spectrum_ref,
+    spectrum_hbm,
     solution_ref,
     residual_ref,
+    mask_ref,
+    spectrum_ref,
     diag,
     quads,
     right,
@@ -135,7 +137,14 @@
     loads = [
         pltpu.make_async_copy(src, dst, load_sems.at[i])
         for i, (src, dst) in enumerate(
-            ((right_hbm, right), (basis_hbm, basis), (quads_hbm, quads), (diag_hbm, diag))
+            (
+                (right_hbm, right),
+                (basis_hbm, basis),
+                (quads_hbm, quads),
+                (mask_hbm, mask_ref),
+                (diag_hbm, diag),
+                (spectrum_hbm, spectrum_ref),
+            )
         )
     ]
     for load in loads:
@@ -294,6 +303,7 @@
     basis_lo[...] = low
     put_part(0, coeff_part(residual))
     loads[2].wait()
+    loads[3].wait()
     for m in range(2):
         for j in range(2):
             keep = mask_ref[m, 0, j].astype(F32)
@@ -303,7 +313,8 @@
 
     spread(0)
     quad_copy(1).start()
-    loads[3].wait()
+    loads[4].wait()
+    loads[5].wait()
 
     centre = 0.5 * (UPPER + LOWER)
     radius = 0.5 * (UPPER - LOWER)
@@ -362,16 +373,17 @@
 def on_device(kernel_diag, pair_quads, tile_mask, right_side, basis, spectrum):
     any_spec = pl.BlockSpec(memory_space=pl.ANY)
     vmem_spec = pl.BlockSpec(memory_space=pltpu.VMEM)
-    smem_spec = pl.BlockSpec(memory_space=pltpu.SMEM)
     out = pltpu.VMEM((RHS, ROWS), F32)
     dma = pltpu.SemaphoreType.DMA
     solved, left = pl.pallas_call(
         body,
         name="chebyshev",
         out_shape=(out, out),
-        in_specs=[smem_spec, any_spec, any_spec, any_spec, any_spec, vmem_spec],
+        in_specs=[any_spec] * 6,
         out_specs=(vmem_spec, vmem_spec),
         scratch_shapes=[
+            pltpu.SMEM((2, 1, 2), jnp.int32),
+            pltpu.VMEM((1, RANK), F32),
             pltpu.VMEM((ROWS, ROWS), BF16),
             pltpu.VMEM((2, ROWS, HALF), BF16),
             pltpu.VMEM((RHS, ROWS), F32),
@@ -392,7 +404,7 @@
             pltpu.VMEM((ITERS, RING, *PIECE), RING_TYPE),
             pltpu.VMEM((ITERS, *PIECE), GATHER_TYPE),
             pltpu.VMEM((ITERS, PLANE, *PIECE), GATHER_TYPE),
-            dma((4,)),
+            dma((6,)),
             dma((2,)),
             dma((2,)),
             dma((2,)),

time: 66 us -> 65.2 us (0.988)
  Pallas kernels: 63.9 us -> 63.2 us
    pallas_call x1, Pallas kernels: 63.9 us -> 63.2 us  [on_device(): pl.pallas_call(body, name='chebyshev', out_shape=(out, out), in_specs=[an...]
where the time goes in v8:
time: 65.2 us; the launch traced here: 65.1 us
  Pallas kernels  63.2 us (97%)
  local copies, waits for them, and re-layouts  1.26 us (2%)
    pallas_call x1, Pallas kernels, on_device(): pl.pallas_call(body, name='chebyshev', out_shape=(out, out), in_specs=[an...  63.2 us

profile of v8, /device:TPU:1, one launch (start us, length us, event | category | flops | bytes accessed | tf_op | source)
XLA Modules:
  0.0 65.1 jit_solution(4726796267555143937)
XLA Ops:
  0.6 63.2 %chebyshev.1 = (f32[64,256]{1,0:T(8,128)S(1)}, f32[64,256]{1,0:T(8,128)S(1)}) custom-call(s32[2,1,2]{2,1,0:T(1,128)} %bitcast.10, bf16[256,256]{1,0:T(8,128)(2,1)} %diag_hbm.1, bf16[2,256,128]{2,1,0:T(8,128)(2,1)} %quads_hbm.1, f32[64,256]{1,0:T(8,128)} %bitcast.9, f32[256,256]{1,0:T(8,128)} %basis_hbm.1, f32[1,256]{1,0:T(1,128)} %bitcast.11), custom_call_target="tpu_custom_call" | custom-call | tf_op jit(solution)/shard_map/chebyshev/pallas_call | solution.py:378
  63.8 0.6 copy.11
  64.5 0.6 copy.12
